TPU v7x, 512 devices: a whole 4x8x8 slice. The times are simulated.
512 devices in a mesh: gs: 128 (over y, z, core), view: 4 (over x).
Axes of the slice: x: 4, y: 8, z: 8, core: 2. Of those that a mesh axis runs over, the one named last changes fastest.
Arguments:
- features: bfloat16 [131072, 128], P('gs'), may hold values from -6 to 6
- geometry: float32 [4, 9, 131072], P('view', None, 'gs'), as said below
- decoder: bfloat16 [128, 512], replicated, may hold values from -0.5 to 0.5
- teacher: bfloat16 [4, 131072, 512], P('view', 'gs'), may hold values from -3 to 3
- images: float32 [4, 3, 131072], P('view', None, 'gs'), may hold values from 0 to 1
- send_index: int32 [4, 128, 1024], P('view', 'gs'), may hold values from 0 to 1023, as said below
- tile_lists: int32 [4, 512, 8], P('view', 'gs'), may hold values from 0 to 7, as said below
- tile_lengths: int32 [4, 512], P('view', 'gs'), may hold values from 2 to 8
Outputs:
- feature_grad: float32 [131072, 128], P(('gs', 'view'))
- geometry_grad: float32 [4, 9, 131072], P('view', None, 'gs')
- decoder_grad: float32 [128, 512], replicated
Inputs may be any that keep to these rules, and one draw needn't show every extreme that they name: `send_index`: each row (one view, one source device) is a permutation of 0 .. 1023; positions k * 8 to (k + 1) * 8 - 1 hold the Gaussians sent to the device of gs index k. `tile_lists`: the 8 entries of a row are distinct. `geometry`: opacity logits lie in -7.5 .. -4, log conics between -2 log 16 and -2 log 16 + 2 log 4, shears in -2 .. 2, colors in 0 .. 1.
All inputs are finite; a program needn't handle non-finite values.
Results may differ from a plain program's by a relative error of at most 0.0017.
Values may be sent and summed in bfloat16 or wider, within the bound.
A program may use at most 64 MiB of HBM per device.

v0:
```python
import math
import jax
import jax.numpy as jnp
from jax import lax
from jax.sharding import PartitionSpec as P

FEAT = 128
CT = 512
TS = 16
BLK = 128
LIST = 8


def composite(tile_geo, alive_mask, pixel_x, pixel_y):
    delta_x = pixel_x[:, None] - tile_geo[0][None, :]
    delta_y = pixel_y[:, None] - tile_geo[1][None, :]
    conic_a = jnp.exp(tile_geo[2])
    conic_c = jnp.exp(tile_geo[3])
    conic_b = 0.8 * jnp.tanh(tile_geo[4]) * jnp.exp(0.5 * (tile_geo[2] + tile_geo[3]))
    exponent = -0.5 * (
        conic_a * delta_x * delta_x
        + 2.0 * conic_b * delta_x * delta_y
        + conic_c * delta_y * delta_y
    )
    opacity = alive_mask * jax.nn.sigmoid(tile_geo[5])
    alpha_val = opacity[None, :] * jnp.exp(exponent)
    log_keep = jnp.log1p(-alpha_val)
    pixel_count = pixel_x.shape[0]
    blocked = log_keep.reshape(pixel_count, LIST, BLK)
    inner = jnp.cumsum(blocked, axis=2) - blocked
    block_sums = jnp.sum(blocked, axis=2)
    outer = jnp.cumsum(block_sums, axis=1) - block_sums
    before = (inner + outer[:, :, None]).reshape(pixel_count, LIST * BLK)
    weights = alpha_val * jnp.exp(before)
    pixel_color = jnp.einsum("pi,ci->cp", weights, tile_geo[6:9], precision=lax.Precision.HIGHEST)
    return (weights, pixel_color)


def device_terms(
    recv_geo, recv_feat, decoder, teacher_dev, images_dev, lists, lengths, shard_index
):
    nblocks = recv_feat.shape[0] // BLK
    tile_pixels = TS * TS
    geo_blocks = recv_geo.reshape(9, nblocks, BLK)
    feat_blocks = recv_feat.reshape(nblocks, BLK, FEAT)
    within = jnp.arange(tile_pixels, dtype=jnp.int32)
    block_range = jnp.arange(nblocks, dtype=jnp.int32)
    slot_range = jnp.arange(LIST, dtype=jnp.int32)

    def tile_step(totals, tile_index):
        decoder_sum, geo_acc, feat_acc = totals
        block_ids = lists[tile_index]
        count = lengths[tile_index]
        alive_mask = jnp.broadcast_to(
            (slot_range < count).astype(jnp.float32)[:, None], (LIST, BLK)
        ).reshape(LIST * BLK)
        tile_geo = jnp.take(geo_blocks, block_ids, axis=1).reshape(9, LIST * BLK)
        feat_tile = jnp.take(feat_blocks, block_ids, axis=0).reshape(LIST * BLK, FEAT)
        column = 2 * TS * (shard_index % 30) + TS * (tile_index % 2) + within % TS
        row_index = 2 * TS * (shard_index // 30) + TS * (tile_index // 2) + within // TS
        pixel_x = column.astype(jnp.float32) + 0.5
        pixel_y = row_index.astype(jnp.float32) + 0.5
        (weights, pixel_color), pullback = jax.vjp(
            lambda geo_part: composite(geo_part, alive_mask, pixel_x, pixel_y), tile_geo
        )
        weight_b = weights.astype(jnp.bfloat16)
        rendered = jnp.dot(weight_b, feat_tile, preferred_element_type=jnp.float32).astype(
            jnp.bfloat16
        )
        pred = jnp.dot(rendered, decoder, preferred_element_type=jnp.float32)
        teacher_rows = lax.dynamic_slice_in_dim(
            teacher_dev, tile_index * tile_pixels, tile_pixels, 0
        )
        error_feat = pred - teacher_rows.astype(jnp.float32)
        gpred = (error_feat / jnp.sqrt(error_feat * error_feat + 0.04)).astype(jnp.bfloat16)
        grender = lax.dot_general(
            gpred, decoder, (((1,), (1,)), ((), ())), preferred_element_type=jnp.float32
        ).astype(jnp.bfloat16)
        decoder_sum = decoder_sum + lax.dot_general(
            rendered, gpred, (((0,), (0,)), ((), ())), preferred_element_type=jnp.float32
        )
        image_cols = lax.dynamic_slice_in_dim(images_dev, tile_index * tile_pixels, tile_pixels, 1)
        error_color = pixel_color - image_cols
        gcolor = error_color / jnp.sqrt(error_color * error_color + 0.04)
        gweight = lax.dot_general(
            grender, feat_tile, (((1,), (1,)), ((), ())), preferred_element_type=jnp.float32
        )
        gfeat_tile = lax.dot_general(
            weight_b, grender, (((0,), (0,)), ((), ())), preferred_element_type=jnp.float32
        )
        (ggeo_tile,) = pullback((gweight, gcolor))
        hits = (block_ids[:, None] == block_range[None, :]).astype(jnp.float32)
        geo_acc = geo_acc + jnp.einsum(
            "clb,ln->cnb", ggeo_tile.reshape(9, LIST, BLK), hits, precision=lax.Precision.HIGHEST
        )
        feat_acc = feat_acc + jnp.einsum(
            "ln,lbf->nbf",
            hits,
            gfeat_tile.reshape(LIST, BLK, FEAT),
            precision=lax.Precision.HIGHEST,
        )
        return ((decoder_sum, geo_acc, feat_acc), None)

    start_totals = (
        jnp.zeros((FEAT, CT), jnp.float32),
        jnp.zeros((9, nblocks, BLK), jnp.float32),
        jnp.zeros((nblocks, BLK, FEAT), jnp.float32),
    )
    tile_range = jnp.arange(lists.shape[0], dtype=jnp.int32)
    (decoder_sum, geo_acc, feat_acc), _ = lax.scan(tile_step, start_totals, tile_range)
    return (decoder_sum, geo_acc.reshape(9, nblocks * BLK), feat_acc.reshape(nblocks * BLK, FEAT))


def on_device(features, geometry, decoder, teacher, images, send_index, tile_lists, tile_lengths):
    send_order = send_index[0, 0]
    shard_index = lax.axis_index("gs")
    geo_send = jnp.take(geometry[0], send_order, axis=1)
    recv_geo = lax.all_to_all(geo_send, "gs", split_axis=1, concat_axis=1, tiled=True)
    feat_send = jnp.take(features, send_order, axis=0)
    recv_feat = lax.all_to_all(feat_send, "gs", split_axis=0, concat_axis=0, tiled=True)
    decoder_sum, geo_acc, feat_acc = device_terms(
        recv_geo,
        recv_feat,
        decoder,
        teacher[0],
        images[0],
        tile_lists[0],
        tile_lengths[0],
        shard_index,
    )
    returned_geo = lax.all_to_all(geo_acc, "gs", split_axis=1, concat_axis=1, tiled=True)
    returned_feat = lax.all_to_all(feat_acc, "gs", split_axis=0, concat_axis=0, tiled=True)
    geo_own = jnp.zeros_like(returned_geo).at[:, send_order].set(returned_geo)
    feat_own = jnp.zeros_like(returned_feat).at[send_order].set(returned_feat)
    quarter = feat_own.shape[0] // lax.axis_size("view")
    summed = lax.psum(feat_own, "view")
    feature_grad = lax.dynamic_slice_in_dim(summed, lax.axis_index("view") * quarter, quarter, 0)
    pixel_total = lax.axis_size("gs") * lax.axis_size("view") * tile_lists.shape[1] * TS * TS
    decoder_grad = lax.psum(decoder_sum, ("gs", "view")) * (1.0 / math.sqrt(pixel_total))
    return (feature_grad, geo_own[None], decoder_grad)


def solution(mesh):
    placed = (
        P("gs", None),
        P("view", None, "gs"),
        P(),
        P("view", "gs", None),
        P("view", None, "gs"),
        P("view", "gs", None),
        P("view", "gs", None),
        P("view", "gs"),
    )
    return jax.shard_map(
        on_device,
        mesh=mesh,
        in_specs=placed,
        out_specs=(P(("gs", "view"), None), P("view", None, "gs"), P()),
        check_vma=False,
    )
```

profile of v0, /device:TPU:8, one launch (start us, length us, event | category | flops | bytes accessed | tf_op | source)
XLA Modules:
  0.0 610.4 jit_solution(10011325874883574381)
XLA Ops:
  10.2 2.8 gather_fusion.2
  14.1 17.4 %all-to-all-start = ((f32[9,128,8]{0,2,1:T(8,128)}), f32[9,128,8]{0,2,1:T(8,128)S(1)}, u32[]{:S(2)}, u32[]{:S(2)}) async-start(f32[9,128,8]{0,2,1:T(8,128)} %bitcast_select_fusion.1), calls=%async_computation | async-start | bytes 1048576 | tf_op jit(solution)/shard_map/all_to_all | solution.py:118
  31.5 3.2 gather_fusion.3
  35.6 16.2 %all-to-all-done = f32[9,128,8]{0,2,1:T(8,128)S(1)} async-done(((f32[9,128,8]{0,2,1:T(8,128)}), f32[9,128,8]{0,2,1:T(8,128)S(1)}, u32[]{:S(2)}, u32[]{:S(2)}) %all-to-all-start) | async-done | bytes 36896 | tf_op jit(solution)/shard_map/all_to_all | solution.py:118
  51.8 6.5 %all-to-all-start.1 = ((bf16[128,8,128]{2,1,0:T(8,128)(2,1)}), bf16[128,8,128]{2,1,0:T(8,128)(2,1)S(1)}, u32[]{:S(2)}, u32[]{:S(2)}) async-start(bf16[128,8,128]{2,1,0:T(8,128)(2,1)} %bitcast_select_fusion.2), calls=%async_computation.1 | async-start | bytes 524288 | tf_op jit(solution)/shard_map/all_to_all | solution.py:120
  60.4 12.6 %all-to-all-done.1 = bf16[128,8,128]{2,1,0:T(8,128)(2,1)S(1)} async-done(((bf16[128,8,128]{2,1,0:T(8,128)(2,1)}), bf16[128,8,128]{2,1,0:T(8,128)(2,1)S(1)}, u32[]{:S(2)}, u32[]{:S(2)}) %all-to-all-start.1) | async-done | bytes 262176 | tf_op jit(solution)/shard_map/all_to_all | solution.py:120
  73.7 187.1 %while.21 = (s32[]{:T(128)}, f32[128,512]{1,0:T(8,128)}, f32[9,8,128]{2,1,0:T(8,128)}, f32[8,128,128]{2,0,1:T(8,128)}, s32[4]{0:T(128)S(1)}, /*index=5*/s32[4]{0...) while((s32[]{:T(128)}, f32[128,512]{1,0:T(8,128)}, ...), condition=%wide.region_13.14_spmd.clone.clone, body=%wide.region_0.13_spmd.clone.clone.sunk | while | flops 448201472 | bytes 62394652 | solution.py:110
  89.3 2.2 exponential_multiply_fusion.2
  97.1 1.8 fusion.171
  105.5 1.5 copy.140
  107.0 3.4 fusion.167
  110.4 1.5 copy.141
  114.7 2.3 fusion.168
  135.2 2.2 exponential_multiply_fusion.2
  141.6 1.4 rsqrt_multiply_fusion.2
  143.1 1.8 fusion.171
  147.6 2.3 convolution_add_fusion.8
  152.6 1.5 copy.140
  154.0 3.4 fusion.167
  157.4 1.5 copy.141
  161.7 2.3 fusion.168
  182.3 2.2 exponential_multiply_fusion.2
  188.6 1.5 rsqrt_multiply_fusion.2
  190.1 1.8 fusion.171
  194.7 2.3 convolution_add_fusion.8
  199.6 1.5 copy.140
  201.1 3.4 fusion.167
  204.4 1.5 copy.141
  208.8 2.3 fusion.168
  229.3 2.2 exponential_multiply_fusion.2
  235.6 1.5 rsqrt_multiply_fusion.2
  237.1 1.8 fusion.171
  241.7 2.3 convolution_add_fusion.8
  246.6 1.5 copy.140
  248.1 3.4 fusion.167
  251.5 1.5 copy.141
  255.8 2.3 fusion.168
  260.8 1.9 copy.80
  262.7 6.5 %all-to-all-start.2 = ((f32[128,8,128]{2,1,0:T(8,128)}), f32[128,8,128]{2,1,0:T(8,128)S(1)}, u32[]{:S(2)}, u32[]{:S(2)}) async-start(f32[128,8,128]{2,1,0:T(8,128)} %bitcast.11), calls=%async_computation.2 | async-start | bytes 1048576 | tf_op jit(solution)/shard_map/all_to_all | solution.py:132
  270.0 19.5 %all-to-all-done.2 = f32[128,8,128]{2,1,0:T(8,128)S(1)} async-done(((f32[128,8,128]{2,1,0:T(8,128)}), f32[128,8,128]{2,1,0:T(8,128)S(1)}, u32[]{:S(2)}, u32[]{:S(2)}) %all-to-all-start.2) | async-done | bytes 524320 | tf_op jit(solution)/shard_map/all_to_all | solution.py:132
  289.5 4.0 scatter_custom_fusion
  295.4 6.4 %all-to-all-start.3 = ((f32[9,128,8]{0,2,1:T(8,128)}), f32[9,128,8]{0,2,1:T(8,128)S(1)}, u32[]{:S(2)}, u32[]{:S(2)}) async-start(f32[9,128,8]{0,2,1:T(8,128)} %bitcast.13), calls=%async_computation.3 | async-start | bytes 1048576 | tf_op jit(solution)/shard_map/all_to_all | solution.py:131
  301.7 20.4 %all-to-all-done.3 = f32[9,128,8]{0,2,1:T(8,128)S(1)} async-done(((f32[9,128,8]{0,2,1:T(8,128)}), f32[9,128,8]{0,2,1:T(8,128)S(1)}, u32[]{:S(2)}, u32[]{:S(2)}) %all-to-all-start.3) | async-done | bytes 36896 | tf_op jit(solution)/shard_map/all_to_all | solution.py:131
  322.2 3.4 scatter_custom_fusion.1
  326.4 222.5 %all-reduce.14.cloned.1.call-done = f32[128,512]{1,0:T(8,128)} async-done(((f32[128,512]{1,0:T(8,128)}), f32[128,512]{1,0:T(8,128)}) %all-reduce.14.cloned.1.call-update) | async-done | bytes 262160 | tf_op jit(solution)/shard_map/psum | solution.py:139
  548.8 1.7 broadcast_multiply_fusion.2
  550.5 51.4 %all-reduce.12.cloned.1.call-done = f32[1024,128]{1,0:T(8,128)} async-done(((f32[1024,128]{1,0:T(8,128)}), f32[1024,128]{1,0:T(8,128)}) %all-reduce.12.cloned.1.call-update) | async-done | bytes 524304 | tf_op jit(solution)/shard_map/psum | solution.py:136
  602.0 1.6 constant_dynamic-slice_fusion.1
  (501 shorter events, 116.0 us)
Async XLA Ops:
  7.2 24.3 %copy-start = (bf16[1024,128]{1,0:T(8,128)(2,1)S(1)}, bf16[1024,128]{1,0:T(8,128)(2,1)}, u32[]{:S(2)}) copy-start(bf16[1024,128]{1,0:T(8,128)(2,1)} %param.10) | copy-start | bytes 786436
  14.1 37.7 %all-to-all-start = ((f32[9,128,8]{0,2,1:T(8,128)}), f32[9,128,8]{0,2,1:T(8,128)S(1)}, u32[]{:S(2)}, u32[]{:S(2)}) async-start(f32[9,128,8]{0,2,1:T(8,128)} %bitcast_select_fusion.1), calls=%async_computation | async-start | bytes 1048576 | tf_op jit(solution)/shard_map/all_to_all | solution.py:118
  51.8 21.3 %all-to-all-start.1 = ((bf16[128,8,128]{2,1,0:T(8,128)(2,1)}), bf16[128,8,128]{2,1,0:T(8,128)(2,1)S(1)}, u32[]{:S(2)}, u32[]{:S(2)}) async-start(bf16[128,8,128]{2,1,0:T(8,128)(2,1)} %bitcast_select_fusion.2), calls=%async_computation.1 | async-start | bytes 524288 | tf_op jit(solution)/shard_map/all_to_all | solution.py:120
  73.7 13.7 %copy-start.8 = (bf16[8,128,128]{2,1,0:T(8,128)(2,1)}, bf16[8,128,128]{2,1,0:T(8,128)(2,1)S(1)}, u32[]{:S(2)}) copy-start(bf16[8,128,128]{2,1,0:T(8,128)(2,1)S(1)} %get-tuple-element.843) | copy-start | bytes 786436 | tf_op jit(solution)/shard_map/while
  81.3 22.9 %copy-start.21 = (f32[256]{0:T(256)}, f32[256]{0:T(256)S(1)}, u32[]{:S(2)}) copy-start(f32[256]{0:T(256)S(1)} %get-tuple-element.768) | copy-start | bytes 3076 | tf_op jit(solution)/shard_map/while
  81.3 22.9 %copy-start.23 = (f32[256]{0:T(256)}, f32[256]{0:T(256)S(1)}, u32[]{:S(2)}) copy-start(f32[256]{0:T(256)S(1)} %get-tuple-element.765) | copy-start | bytes 3076 | tf_op jit(solution)/shard_map/while
  82.0 19.6 %copy-start.28 = (s32[8]{0:T(128)}, s32[8]{0:T(128)S(1)}, u32[]{:S(2)}) copy-start(s32[8]{0:T(128)S(1)} %get-tuple-element.785) | copy-start | bytes 100 | tf_op jit(solution)/shard_map/while
  84.2 18.9 %copy-start.5 = (f32[9,8,128]{2,0,1:T(8,128)}, f32[9,8,128]{2,0,1:T(8,128)S(1)}, u32[]{:S(2)}) copy-start(f32[9,8,128]{2,0,1:T(8,128)S(1)} %select_bitcast_fusion.2) | copy-start | bytes 110596 | tf_op jit(solution)/shard_map/while
  84.9 19.4 %copy-start.11 = (f32[1,8,128]{2,0,1:T(1,128)}, f32[1,8,128]{2,0,1:T(1,128)S(1)}, u32[]{:S(2)}) copy-start(f32[1,8,128]{2,0,1:T(1,128)S(1)} %get-tuple-element.769) | copy-start | bytes 12292 | tf_op jit(solution)/shard_map/while
  85.5 18.8 %copy-start.16 = (f32[1024]{0:T(1024)}, f32[1024]{0:T(1024)S(1)}, u32[]{:S(2)}) copy-start(f32[1024]{0:T(1024)S(1)} %bitcast_multiply_fusion.8) | copy-start | bytes 12292 | tf_op jit(solution)/shard_map/while
  114.7 2.4 copy-start.27
  114.7 3.3 copy-start.25
  117.0 2.6 copy-start.9
  119.6 13.7 %copy-start.8 = (bf16[8,128,128]{2,1,0:T(8,128)(2,1)}, bf16[8,128,128]{2,1,0:T(8,128)(2,1)S(1)}, u32[]{:S(2)}) copy-start(bf16[8,128,128]{2,1,0:T(8,128)(2,1)S(1)} %get-tuple-element.843) | copy-start | bytes 786436 | tf_op jit(solution)/shard_map/while
  127.3 24.0 %copy-start.21 = (f32[256]{0:T(256)}, f32[256]{0:T(256)S(1)}, u32[]{:S(2)}) copy-start(f32[256]{0:T(256)S(1)} %get-tuple-element.768) | copy-start | bytes 3076 | tf_op jit(solution)/shard_map/while
  127.3 24.0 %copy-start.23 = (f32[256]{0:T(256)}, f32[256]{0:T(256)S(1)}, u32[]{:S(2)}) copy-start(f32[256]{0:T(256)S(1)} %get-tuple-element.765) | copy-start | bytes 3076 | tf_op jit(solution)/shard_map/while
  128.0 19.6 %copy-start.28 = (s32[8]{0:T(128)}, s32[8]{0:T(128)S(1)}, u32[]{:S(2)}) copy-start(s32[8]{0:T(128)S(1)} %get-tuple-element.785) | copy-start | bytes 100 | tf_op jit(solution)/shard_map/while
  130.2 20.0 %copy-start.5 = (f32[9,8,128]{2,0,1:T(8,128)}, f32[9,8,128]{2,0,1:T(8,128)S(1)}, u32[]{:S(2)}) copy-start(f32[9,8,128]{2,0,1:T(8,128)S(1)} %select_bitcast_fusion.2) | copy-start | bytes 110596 | tf_op jit(solution)/shard_map/while
  130.8 20.5 %copy-start.11 = (f32[1,8,128]{2,0,1:T(1,128)}, f32[1,8,128]{2,0,1:T(1,128)S(1)}, u32[]{:S(2)}) copy-start(f32[1,8,128]{2,0,1:T(1,128)S(1)} %get-tuple-element.769) | copy-start | bytes 12292 | tf_op jit(solution)/shard_map/while
  131.4 19.9 %copy-start.16 = (f32[1024]{0:T(1024)}, f32[1024]{0:T(1024)S(1)}, u32[]{:S(2)}) copy-start(f32[1024]{0:T(1024)S(1)} %bitcast_multiply_fusion.8) | copy-start | bytes 12292 | tf_op jit(solution)/shard_map/while
  147.3 2.6 copy-start.7
  161.7 2.4 copy-start.27
  161.7 3.3 copy-start.25
  164.0 2.6 copy-start.9
  166.6 13.7 %copy-start.8 = (bf16[8,128,128]{2,1,0:T(8,128)(2,1)}, bf16[8,128,128]{2,1,0:T(8,128)(2,1)S(1)}, u32[]{:S(2)}) copy-start(bf16[8,128,128]{2,1,0:T(8,128)(2,1)S(1)} %get-tuple-element.843) | copy-start | bytes 786436 | tf_op jit(solution)/shard_map/while
  174.3 24.0 %copy-start.21 = (f32[256]{0:T(256)}, f32[256]{0:T(256)S(1)}, u32[]{:S(2)}) copy-start(f32[256]{0:T(256)S(1)} %get-tuple-element.768) | copy-start | bytes 3076 | tf_op jit(solution)/shard_map/while
  174.3 24.0 %copy-start.23 = (f32[256]{0:T(256)}, f32[256]{0:T(256)S(1)}, u32[]{:S(2)}) copy-start(f32[256]{0:T(256)S(1)} %get-tuple-element.765) | copy-start | bytes 3076 | tf_op jit(solution)/shard_map/while
  175.0 19.6 %copy-start.28 = (s32[8]{0:T(128)}, s32[8]{0:T(128)S(1)}, u32[]{:S(2)}) copy-start(s32[8]{0:T(128)S(1)} %get-tuple-element.785) | copy-start | bytes 100 | tf_op jit(solution)/shard_map/while
  177.2 20.0 %copy-start.5 = (f32[9,8,128]{2,0,1:T(8,128)}, f32[9,8,128]{2,0,1:T(8,128)S(1)}, u32[]{:S(2)}) copy-start(f32[9,8,128]{2,0,1:T(8,128)S(1)} %select_bitcast_fusion.2) | copy-start | bytes 110596 | tf_op jit(solution)/shard_map/while
  177.8 20.5 %copy-start.11 = (f32[1,8,128]{2,0,1:T(1,128)}, f32[1,8,128]{2,0,1:T(1,128)S(1)}, u32[]{:S(2)}) copy-start(f32[1,8,128]{2,0,1:T(1,128)S(1)} %get-tuple-element.769) | copy-start | bytes 12292 | tf_op jit(solution)/shard_map/while
  178.4 19.9 %copy-start.16 = (f32[1024]{0:T(1024)}, f32[1024]{0:T(1024)S(1)}, u32[]{:S(2)}) copy-start(f32[1024]{0:T(1024)S(1)} %bitcast_multiply_fusion.8) | copy-start | bytes 12292 | tf_op jit(solution)/shard_map/while
  194.3 2.6 copy-start.7
  208.7 3.3 copy-start.25
  211.0 2.6 copy-start.9
  213.7 13.7 %copy-start.8 = (bf16[8,128,128]{2,1,0:T(8,128)(2,1)}, bf16[8,128,128]{2,1,0:T(8,128)(2,1)S(1)}, u32[]{:S(2)}) copy-start(bf16[8,128,128]{2,1,0:T(8,128)(2,1)S(1)} %get-tuple-element.843) | copy-start | bytes 786436 | tf_op jit(solution)/shard_map/while
  221.3 24.0 %copy-start.21 = (f32[256]{0:T(256)}, f32[256]{0:T(256)S(1)}, u32[]{:S(2)}) copy-start(f32[256]{0:T(256)S(1)} %get-tuple-element.768) | copy-start | bytes 3076 | tf_op jit(solution)/shard_map/while
  221.3 24.0 %copy-start.23 = (f32[256]{0:T(256)}, f32[256]{0:T(256)S(1)}, u32[]{:S(2)}) copy-start(f32[256]{0:T(256)S(1)} %get-tuple-element.765) | copy-start | bytes 3076 | tf_op jit(solution)/shard_map/while
  222.0 19.6 %copy-start.28 = (s32[8]{0:T(128)}, s32[8]{0:T(128)S(1)}, u32[]{:S(2)}) copy-start(s32[8]{0:T(128)S(1)} %get-tuple-element.785) | copy-start | bytes 100 | tf_op jit(solution)/shard_map/while
  224.2 20.0 %copy-start.5 = (f32[9,8,128]{2,0,1:T(8,128)}, f32[9,8,128]{2,0,1:T(8,128)S(1)}, u32[]{:S(2)}) copy-start(f32[9,8,128]{2,0,1:T(8,128)S(1)} %select_bitcast_fusion.2) | copy-start | bytes 110596 | tf_op jit(solution)/shard_map/while
  224.9 20.5 %copy-start.11 = (f32[1,8,128]{2,0,1:T(1,128)}, f32[1,8,128]{2,0,1:T(1,128)S(1)}, u32[]{:S(2)}) copy-start(f32[1,8,128]{2,0,1:T(1,128)S(1)} %get-tuple-element.769) | copy-start | bytes 12292 | tf_op jit(solution)/shard_map/while
  225.5 19.9 %copy-start.16 = (f32[1024]{0:T(1024)}, f32[1024]{0:T(1024)S(1)}, u32[]{:S(2)}) copy-start(f32[1024]{0:T(1024)S(1)} %bitcast_multiply_fusion.8) | copy-start | bytes 12292 | tf_op jit(solution)/shard_map/while
  241.4 2.6 copy-start.7
  255.8 3.3 copy-start.25
  258.1 2.6 copy-start.9
  262.7 26.8 %all-to-all-start.2 = ((f32[128,8,128]{2,1,0:T(8,128)}), f32[128,8,128]{2,1,0:T(8,128)S(1)}, u32[]{:S(2)}, u32[]{:S(2)}) async-start(f32[128,8,128]{2,1,0:T(8,128)} %bitcast.11), calls=%async_computation.2 | async-start | bytes 1048576 | tf_op jit(solution)/shard_map/all_to_all | solution.py:132
  269.2 279.6 %all-reduce.14.cloned.1.call-start = ((), (), s32[]{:S(2)}) async-start(), calls=%async_computation.5 | async-start | bytes 524288 | tf_op jit(solution)/shard_map/psum | solution.py:139
  269.9 332.0 %all-reduce.12.cloned.1.call-start = ((), (), s32[]{:S(2)}) async-start(), calls=%async_computation.4 | async-start | bytes 1048576 | tf_op jit(solution)/shard_map/psum | solution.py:136
  295.4 26.8 %all-to-all-start.3 = ((f32[9,128,8]{0,2,1:T(8,128)}), f32[9,128,8]{0,2,1:T(8,128)S(1)}, u32[]{:S(2)}, u32[]{:S(2)}) async-start(f32[9,128,8]{0,2,1:T(8,128)} %bitcast.13), calls=%async_computation.3 | async-start | bytes 1048576 | tf_op jit(solution)/shard_map/all_to_all | solution.py:131
  (89 other events, 104.6 us)
Sparse Core Ops, SparseCore 0:
  275.6 273.1 all-reduce.13
  551.3 50.6 all-reduce.11
where the time goes:
time: 613 us; the launch traced here: 610 us
  waiting for transfers between devices  343 us (56%)
  local copies, waits for them, and re-layouts  79.9 us (13%)
  other arithmetic  76.6 us (12%)
  matrix products  39.1 us (6%)
  starting transfers between devices  36.8 us (6%)
  loops' own time  20.3 us (3%)
  between operations  14.3 us (2%)
    psum x1, waiting for transfers between devices, on_device(): lax.psum(decoder_sum, ('gs', 'view')) * (1.0 / math.sqrt(pixel_total))  222 us
    psum x1, waiting for transfers between devices, on_device(): summed = lax.psum(feat_own, 'view')  51.4 us
    another operation x8, other arithmetic, composite(): inner = jnp.cumsum(blocked, axis=2) - blocked  22.4 us
    all_to_all x1, waiting for transfers between devices, on_device(): lax.all_to_all(geo_acc, 'gs', split_axis=1, concat_axis=1, tiled=True)  20.4 us
    another operation x1, loops' own time, device_terms(): lax.scan(tile_step, start_totals, tile_range)  20.3 us
    all_to_all x1, waiting for transfers between devices, on_device(): lax.all_to_all(feat_acc, 'gs', split_axis=0, concat_axis=0, tiled=True)  19.5 us
    while x264, local copies, waits for them, and re-layouts  19.3 us
    all_to_all x1, starting transfers between devices, on_device(): lax.all_to_all(geo_send, 'gs', split_axis=1, concat_axis=1, tiled=True)  17.4 us
  transfers between devices with their start and end apart: 6, of which 6 were waited for; matrix products, arithmetic and copies ran while one was open for 3% of the time, Pallas kernels for 0%

commit v1 on v0

--- a/solution.py
+++ b/solution.py
@@ -133,7 +133,11 @@
     geo_own = jnp.zeros_like(returned_geo).at[:, send_order].set(returned_geo)
     feat_own = jnp.zeros_like(returned_feat).at[send_order].set(returned_feat)
     quarter = feat_own.shape[0] // lax.axis_size("view")
-    summed = lax.psum(feat_own, "view")
+    size = lax.axis_size("view")
+    summed, far = (feat_own, 1)
+    while far < size:
+        summed = summed + lax.ppermute(summed, "view", [(i, i ^ far) for i in range(size)])
+        far = 2 * far
     feature_grad = lax.dynamic_slice_in_dim(summed, lax.axis_index("view") * quarter, quarter, 0)
     pixel_total = lax.axis_size("gs") * lax.axis_size("view") * tile_lists.shape[1] * TS * TS
     decoder_grad = lax.psum(decoder_sum, ("gs", "view")) * (1.0 / math.sqrt(pixel_total))

time: 613 us -> 586 us (0.956)
  the two profiles are of different devices: /device:TPU:8 before, /device:TPU:23 now
where the time goes in v1:
time: 586 us; the launch traced here: 583 us
  waiting for transfers between devices  292 us (50%)
  other arithmetic  77.3 us (13%)
  local copies, waits for them, and re-layouts  73 us (12%)
  starting transfers between devices  41.9 us (7%)
  matrix products  39.3 us (7%)
  blocking collectives  25.3 us (4%)
  loops' own time  20.6 us (4%)
  between operations  14.3 us (2%)
    psum x1, waiting for transfers between devices, on_device(): lax.psum(decoder_sum, ('gs', 'view')) * (1.0 / math.sqrt(pixel_total))  237 us
    all_to_all x1, blocking collectives, on_device(): lax.all_to_all(feat_acc, 'gs', split_axis=0, concat_axis=0, tiled=True)  25.3 us
    another operation x8, other arithmetic, composite(): inner = jnp.cumsum(blocked, axis=2) - blocked  22.4 us
    another operation x1, loops' own time, device_terms(): lax.scan(tile_step, start_totals, tile_range)  20.6 us
    while x280, local copies, waits for them, and re-layouts  19.2 us
    all_to_all x1, waiting for transfers between devices, on_device(): lax.all_to_all(geo_acc, 'gs', split_axis=1, concat_axis=1, tiled=True)  18 us
    all_to_all x1, starting transfers between devices, on_device(): lax.all_to_all(geo_send, 'gs', split_axis=1, concat_axis=1, tiled=True)  17.7 us
    dot_general x12, matrix products, composite(): jnp.einsum('pi,ci->cp', weights, tile_geo[6:9], precision=lax.Precision.H...  17.3 us
  transfers between devices with their start and end apart: 6, of which 5 were waited for; matrix products, arithmetic and copies ran while one was open for 2% of the time, Pallas kernels for 0%

profile of v1, /device:TPU:23, one launch (start us, length us, event | category | flops | bytes accessed | tf_op | source)
XLA Modules:
  0.0 583.4 jit_solution(10601757120363102289)
XLA Ops:
  10.2 2.8 gather_fusion.2
  14.1 17.7 %all-to-all-start = ((f32[9,128,8]{0,2,1:T(8,128)}), f32[9,128,8]{0,2,1:T(8,128)S(1)}, u32[]{:S(2)}, u32[]{:S(2)}) async-start(f32[9,128,8]{0,2,1:T(8,128)} %bitcast_select_fusion.1), calls=%async_computation | async-start | bytes 1048576 | tf_op jit(solution)/shard_map/all_to_all | solution.py:118
  31.7 3.2 gather_fusion.3
  35.9 13.8 %all-to-all-done = f32[9,128,8]{0,2,1:T(8,128)S(1)} async-done(((f32[9,128,8]{0,2,1:T(8,128)}), f32[9,128,8]{0,2,1:T(8,128)S(1)}, u32[]{:S(2)}, u32[]{:S(2)}) %all-to-all-start) | async-done | bytes 36896 | tf_op jit(solution)/shard_map/all_to_all | solution.py:118
  49.6 8.9 %all-to-all-start.1 = ((bf16[128,8,128]{2,1,0:T(8,128)(2,1)}), bf16[128,8,128]{2,1,0:T(8,128)(2,1)S(1)}, u32[]{:S(2)}, u32[]{:S(2)}) async-start(bf16[128,8,128]{2,1,0:T(8,128)(2,1)} %bitcast_select_fusion.2), calls=%async_computation.1 | async-start | bytes 524288 | tf_op jit(solution)/shard_map/all_to_all | solution.py:120
  60.1 11.6 %all-to-all-done.1 = bf16[128,8,128]{2,1,0:T(8,128)(2,1)S(1)} async-done(((bf16[128,8,128]{2,1,0:T(8,128)(2,1)}), bf16[128,8,128]{2,1,0:T(8,128)(2,1)S(1)}, u32[]{:S(2)}, u32[]{:S(2)}) %all-to-all-start.1) | async-done | bytes 262176 | tf_op jit(solution)/shard_map/all_to_all | solution.py:120
  72.3 184.3 %while.21 = (s32[]{:T(128)}, f32[128,512]{1,0:T(8,128)}, f32[9,8,128]{2,1,0:T(8,128)}, f32[8,128,128]{2,0,1:T(8,128)}, s32[4]{0:T(128)S(1)}, /*index=5*/s32[4]{0...) while((s32[]{:T(128)}, f32[128,512]{1,0:T(8,128)}, ...), condition=%wide.region_13.14_spmd.clone.clone, body=%wide.region_0.13_spmd.clone.clone.sunk | while | flops 448201472 | bytes 62689620 | solution.py:110
  87.2 2.2 exponential_multiply_fusion.2
  93.6 1.4 rsqrt_multiply_fusion.2
  95.0 1.8 fusion.171
  103.5 1.5 copy.140
  105.0 3.4 fusion.167
  108.4 1.5 copy.141
  112.6 2.3 fusion.168
  132.4 2.2 exponential_multiply_fusion.2
  138.8 1.4 rsqrt_multiply_fusion.2
  140.2 1.8 fusion.171
  144.8 2.3 convolution_add_fusion.8
  149.8 1.5 copy.140
  151.3 3.4 fusion.167
  154.6 1.5 copy.141
  158.9 2.3 fusion.168
  178.7 2.2 exponential_multiply_fusion.2
  185.1 1.5 rsqrt_multiply_fusion.2
  186.5 1.8 fusion.171
  191.1 2.3 convolution_add_fusion.8
  196.1 1.5 copy.140
  197.6 3.4 fusion.167
  200.9 1.5 copy.141
  205.2 2.3 fusion.168
  225.0 2.2 exponential_multiply_fusion.2
  231.3 1.5 rsqrt_multiply_fusion.2
  232.8 1.8 fusion.171
  237.4 2.3 convolution_add_fusion.8
  242.4 1.5 copy.140
  243.9 3.4 fusion.167
  247.2 1.5 copy.141
  251.5 2.3 fusion.168
  257.8 25.3 %all_to_all.36 = f32[128,8,128]{2,1,0:T(8,128)S(1)} all-to-all(f32[128,8,128]{2,1,0:T(8,128)S(1)} %bitcast.322), channel_id=1, replica_groups=mesh['gs'=128,'view'=4] {'gs'}, dimensions={0} | all-to-all | bytes 1048576 | tf_op jit(solution)/shard_map/all_to_all | solution.py:132
  283.1 3.4 scatter_custom_fusion
  286.5 2.5 collective-permute-start
  288.9 11.8 %collective-permute-done = f32[1024,128]{1,0:T(8,128)S(1)} collective-permute-done((f32[1024,128]{1,0:T(8,128)S(1)}, f32[1024,128]{1,0:T(8,128)S(1)}, u32[]{:S(2)}, u32[]{:S(2)}) %collective-permute-start) | collective-permute-done | bytes 524320 | tf_op jit(solution)/shard_map/ppermute | solution.py:139
  300.8 3.0 collective-permute-start.1
  305.6 9.8 %all-to-all-start.3 = ((f32[9,128,8]{0,2,1:T(8,128)}), f32[9,128,8]{0,2,1:T(8,128)S(1)}, u32[]{:S(2)}, u32[]{:S(2)}) async-start(f32[9,128,8]{0,2,1:T(8,128)} %bitcast.13), calls=%async_computation.3 | async-start | bytes 1048576 | tf_op jit(solution)/shard_map/all_to_all | solution.py:131
  315.5 18.0 %all-to-all-done.3 = f32[9,128,8]{0,2,1:T(8,128)S(1)} async-done(((f32[9,128,8]{0,2,1:T(8,128)}), f32[9,128,8]{0,2,1:T(8,128)S(1)}, u32[]{:S(2)}, u32[]{:S(2)}) %all-to-all-start.3) | async-done | bytes 36896 | tf_op jit(solution)/shard_map/all_to_all | solution.py:131
  333.5 3.4 scatter_custom_fusion.1
  337.7 236.5 %all-reduce.11.cloned.1.call-done = f32[128,512]{1,0:T(8,128)} async-done(((f32[128,512]{1,0:T(8,128)}), f32[128,512]{1,0:T(8,128)}) %all-reduce.11.cloned.1.call-update) | async-done | bytes 262160 | tf_op jit(solution)/shard_map/psum | solution.py:143
  574.2 1.7 broadcast_multiply_fusion.2
  (518 shorter events, 111.8 us)
Async XLA Ops:
  7.2 24.6 %copy-start = (bf16[1024,128]{1,0:T(8,128)(2,1)S(1)}, bf16[1024,128]{1,0:T(8,128)(2,1)}, u32[]{:S(2)}) copy-start(bf16[1024,128]{1,0:T(8,128)(2,1)} %param.10) | copy-start | bytes 786436
  14.1 35.6 %all-to-all-start = ((f32[9,128,8]{0,2,1:T(8,128)}), f32[9,128,8]{0,2,1:T(8,128)S(1)}, u32[]{:S(2)}, u32[]{:S(2)}) async-start(f32[9,128,8]{0,2,1:T(8,128)} %bitcast_select_fusion.1), calls=%async_computation | async-start | bytes 1048576 | tf_op jit(solution)/shard_map/all_to_all | solution.py:118
  49.6 22.1 %all-to-all-start.1 = ((bf16[128,8,128]{2,1,0:T(8,128)(2,1)}), bf16[128,8,128]{2,1,0:T(8,128)(2,1)S(1)}, u32[]{:S(2)}, u32[]{:S(2)}) async-start(bf16[128,8,128]{2,1,0:T(8,128)(2,1)} %bitcast_select_fusion.2), calls=%async_computation.1 | async-start | bytes 524288 | tf_op jit(solution)/shard_map/all_to_all | solution.py:120
  58.5 515.6 %all-reduce.11.cloned.1.call-start = ((), (), s32[]{:S(2)}) async-start(), calls=%async_computation.4 | async-start | bytes 524288 | tf_op jit(solution)/shard_map/psum | solution.py:143
  72.3 10.4 %copy-start.21 = (f32[9,8,128]{2,0,1:T(8,128)}, f32[9,8,128]{2,0,1:T(8,128)S(1)}, u32[]{:S(2)}) copy-start(f32[9,8,128]{2,0,1:T(8,128)S(1)} %get-tuple-element.840) | copy-start | bytes 110596 | tf_op jit(solution)/shard_map/while
  72.3 12.9 %copy-start.8 = (bf16[8,128,128]{2,1,0:T(8,128)(2,1)}, bf16[8,128,128]{2,1,0:T(8,128)(2,1)S(1)}, u32[]{:S(2)}) copy-start(bf16[8,128,128]{2,1,0:T(8,128)(2,1)S(1)} %get-tuple-element.843) | copy-start | bytes 786436 | tf_op jit(solution)/shard_map/while
  80.1 22.1 %copy-start.23 = (f32[256]{0:T(256)}, f32[256]{0:T(256)S(1)}, u32[]{:S(2)}) copy-start(f32[256]{0:T(256)S(1)} %get-tuple-element.768) | copy-start | bytes 3076 | tf_op jit(solution)/shard_map/while
  80.1 22.2 %copy-start.25 = (f32[256]{0:T(256)}, f32[256]{0:T(256)S(1)}, u32[]{:S(2)}) copy-start(f32[256]{0:T(256)S(1)} %get-tuple-element.765) | copy-start | bytes 3076 | tf_op jit(solution)/shard_map/while
  80.8 18.8 %copy-start.30 = (s32[8]{0:T(128)}, s32[8]{0:T(128)S(1)}, u32[]{:S(2)}) copy-start(s32[8]{0:T(128)S(1)} %get-tuple-element.785) | copy-start | bytes 100 | tf_op jit(solution)/shard_map/while
  82.1 19.0 %copy-start.5 = (f32[9,8,128]{2,0,1:T(8,128)}, f32[9,8,128]{2,0,1:T(8,128)S(1)}, u32[]{:S(2)}) copy-start(f32[9,8,128]{2,0,1:T(8,128)S(1)} %select_bitcast_fusion.2) | copy-start | bytes 110596 | tf_op jit(solution)/shard_map/while
  82.8 19.4 %copy-start.11 = (f32[1,8,128]{2,0,1:T(1,128)}, f32[1,8,128]{2,0,1:T(1,128)S(1)}, u32[]{:S(2)}) copy-start(f32[1,8,128]{2,0,1:T(1,128)S(1)} %get-tuple-element.769) | copy-start | bytes 12292 | tf_op jit(solution)/shard_map/while
  83.4 18.9 %copy-start.16 = (f32[1024]{0:T(1024)}, f32[1024]{0:T(1024)S(1)}, u32[]{:S(2)}) copy-start(f32[1024]{0:T(1024)S(1)} %bitcast_multiply_fusion.8) | copy-start | bytes 12292 | tf_op jit(solution)/shard_map/while
  112.6 3.3 copy-start.27
  114.9 2.6 copy-start.9
  117.6 10.4 %copy-start.21 = (f32[9,8,128]{2,0,1:T(8,128)}, f32[9,8,128]{2,0,1:T(8,128)S(1)}, u32[]{:S(2)}) copy-start(f32[9,8,128]{2,0,1:T(8,128)S(1)} %get-tuple-element.840) | copy-start | bytes 110596 | tf_op jit(solution)/shard_map/while
  117.6 12.9 %copy-start.8 = (bf16[8,128,128]{2,1,0:T(8,128)(2,1)}, bf16[8,128,128]{2,1,0:T(8,128)(2,1)S(1)}, u32[]{:S(2)}) copy-start(bf16[8,128,128]{2,1,0:T(8,128)(2,1)S(1)} %get-tuple-element.843) | copy-start | bytes 786436 | tf_op jit(solution)/shard_map/while
  125.3 23.2 %copy-start.23 = (f32[256]{0:T(256)}, f32[256]{0:T(256)S(1)}, u32[]{:S(2)}) copy-start(f32[256]{0:T(256)S(1)} %get-tuple-element.768) | copy-start | bytes 3076 | tf_op jit(solution)/shard_map/while
  125.3 23.2 %copy-start.25 = (f32[256]{0:T(256)}, f32[256]{0:T(256)S(1)}, u32[]{:S(2)}) copy-start(f32[256]{0:T(256)S(1)} %get-tuple-element.765) | copy-start | bytes 3076 | tf_op jit(solution)/shard_map/while
  126.0 18.8 %copy-start.30 = (s32[8]{0:T(128)}, s32[8]{0:T(128)S(1)}, u32[]{:S(2)}) copy-start(s32[8]{0:T(128)S(1)} %get-tuple-element.785) | copy-start | bytes 100 | tf_op jit(solution)/shard_map/while
  127.3 20.1 %copy-start.5 = (f32[9,8,128]{2,0,1:T(8,128)}, f32[9,8,128]{2,0,1:T(8,128)S(1)}, u32[]{:S(2)}) copy-start(f32[9,8,128]{2,0,1:T(8,128)S(1)} %select_bitcast_fusion.2) | copy-start | bytes 110596 | tf_op jit(solution)/shard_map/while
  128.0 20.5 %copy-start.11 = (f32[1,8,128]{2,0,1:T(1,128)}, f32[1,8,128]{2,0,1:T(1,128)S(1)}, u32[]{:S(2)}) copy-start(f32[1,8,128]{2,0,1:T(1,128)S(1)} %get-tuple-element.769) | copy-start | bytes 12292 | tf_op jit(solution)/shard_map/while
  128.6 20.0 %copy-start.16 = (f32[1024]{0:T(1024)}, f32[1024]{0:T(1024)S(1)}, u32[]{:S(2)}) copy-start(f32[1024]{0:T(1024)S(1)} %bitcast_multiply_fusion.8) | copy-start | bytes 12292 | tf_op jit(solution)/shard_map/while
  158.9 3.3 copy-start.27
  161.2 2.6 copy-start.9
  163.8 10.4 %copy-start.21 = (f32[9,8,128]{2,0,1:T(8,128)}, f32[9,8,128]{2,0,1:T(8,128)S(1)}, u32[]{:S(2)}) copy-start(f32[9,8,128]{2,0,1:T(8,128)S(1)} %get-tuple-element.840) | copy-start | bytes 110596 | tf_op jit(solution)/shard_map/while
  163.9 12.9 %copy-start.8 = (bf16[8,128,128]{2,1,0:T(8,128)(2,1)}, bf16[8,128,128]{2,1,0:T(8,128)(2,1)S(1)}, u32[]{:S(2)}) copy-start(bf16[8,128,128]{2,1,0:T(8,128)(2,1)S(1)} %get-tuple-element.843) | copy-start | bytes 786436 | tf_op jit(solution)/shard_map/while
  171.5 23.2 %copy-start.23 = (f32[256]{0:T(256)}, f32[256]{0:T(256)S(1)}, u32[]{:S(2)}) copy-start(f32[256]{0:T(256)S(1)} %get-tuple-element.768) | copy-start | bytes 3076 | tf_op jit(solution)/shard_map/while
  171.5 23.2 %copy-start.25 = (f32[256]{0:T(256)}, f32[256]{0:T(256)S(1)}, u32[]{:S(2)}) copy-start(f32[256]{0:T(256)S(1)} %get-tuple-element.765) | copy-start | bytes 3076 | tf_op jit(solution)/shard_map/while
  172.3 18.8 %copy-start.30 = (s32[8]{0:T(128)}, s32[8]{0:T(128)S(1)}, u32[]{:S(2)}) copy-start(s32[8]{0:T(128)S(1)} %get-tuple-element.785) | copy-start | bytes 100 | tf_op jit(solution)/shard_map/while
  173.6 20.1 %copy-start.5 = (f32[9,8,128]{2,0,1:T(8,128)}, f32[9,8,128]{2,0,1:T(8,128)S(1)}, u32[]{:S(2)}) copy-start(f32[9,8,128]{2,0,1:T(8,128)S(1)} %select_bitcast_fusion.2) | copy-start | bytes 110596 | tf_op jit(solution)/shard_map/while
  174.3 20.5 %copy-start.11 = (f32[1,8,128]{2,0,1:T(1,128)}, f32[1,8,128]{2,0,1:T(1,128)S(1)}, u32[]{:S(2)}) copy-start(f32[1,8,128]{2,0,1:T(1,128)S(1)} %get-tuple-element.769) | copy-start | bytes 12292 | tf_op jit(solution)/shard_map/while
  174.9 20.0 %copy-start.16 = (f32[1024]{0:T(1024)}, f32[1024]{0:T(1024)S(1)}, u32[]{:S(2)}) copy-start(f32[1024]{0:T(1024)S(1)} %bitcast_multiply_fusion.8) | copy-start | bytes 12292 | tf_op jit(solution)/shard_map/while
  205.2 3.3 copy-start.27
  207.5 2.6 copy-start.9
  210.1 10.4 %copy-start.21 = (f32[9,8,128]{2,0,1:T(8,128)}, f32[9,8,128]{2,0,1:T(8,128)S(1)}, u32[]{:S(2)}) copy-start(f32[9,8,128]{2,0,1:T(8,128)S(1)} %get-tuple-element.840) | copy-start | bytes 110596 | tf_op jit(solution)/shard_map/while
  210.1 12.9 %copy-start.8 = (bf16[8,128,128]{2,1,0:T(8,128)(2,1)}, bf16[8,128,128]{2,1,0:T(8,128)(2,1)S(1)}, u32[]{:S(2)}) copy-start(bf16[8,128,128]{2,1,0:T(8,128)(2,1)S(1)} %get-tuple-element.843) | copy-start | bytes 786436 | tf_op jit(solution)/shard_map/while
  217.8 23.2 %copy-start.23 = (f32[256]{0:T(256)}, f32[256]{0:T(256)S(1)}, u32[]{:S(2)}) copy-start(f32[256]{0:T(256)S(1)} %get-tuple-element.768) | copy-start | bytes 3076 | tf_op jit(solution)/shard_map/while
  217.8 23.3 %copy-start.25 = (f32[256]{0:T(256)}, f32[256]{0:T(256)S(1)}, u32[]{:S(2)}) copy-start(f32[256]{0:T(256)S(1)} %get-tuple-element.765) | copy-start | bytes 3076 | tf_op jit(solution)/shard_map/while
  218.5 18.8 %copy-start.30 = (s32[8]{0:T(128)}, s32[8]{0:T(128)S(1)}, u32[]{:S(2)}) copy-start(s32[8]{0:T(128)S(1)} %get-tuple-element.785) | copy-start | bytes 100 | tf_op jit(solution)/shard_map/while
  219.9 20.1 %copy-start.5 = (f32[9,8,128]{2,0,1:T(8,128)}, f32[9,8,128]{2,0,1:T(8,128)S(1)}, u32[]{:S(2)}) copy-start(f32[9,8,128]{2,0,1:T(8,128)S(1)} %select_bitcast_fusion.2) | copy-start | bytes 110596 | tf_op jit(solution)/shard_map/while
  220.6 20.5 %copy-start.11 = (f32[1,8,128]{2,0,1:T(1,128)}, f32[1,8,128]{2,0,1:T(1,128)S(1)}, u32[]{:S(2)}) copy-start(f32[1,8,128]{2,0,1:T(1,128)S(1)} %get-tuple-element.769) | copy-start | bytes 12292 | tf_op jit(solution)/shard_map/while
  221.2 20.0 %copy-start.16 = (f32[1024]{0:T(1024)}, f32[1024]{0:T(1024)S(1)}, u32[]{:S(2)}) copy-start(f32[1024]{0:T(1024)S(1)} %bitcast_multiply_fusion.8) | copy-start | bytes 12292 | tf_op jit(solution)/shard_map/while
  237.1 2.6 copy-start.7
  251.5 3.3 copy-start.27
  253.8 2.6 copy-start.9
  286.5 14.2 %collective-permute-start = (f32[1024,128]{1,0:T(8,128)S(1)}, f32[1024,128]{1,0:T(8,128)S(1)}, u32[]{:S(2)}, u32[]{:S(2)}) collective-permute-start(f32[1024,128]{1,0:T(8,128)S(1)} %scatter_custom_fusion), channel_id=1, source_target_pairs={{0,1},{1,0},{2,3},{3,2},{4,5},{5,4},{6,7},{7,6},{8,9},{9,8},{10,11... | collective-permute-start | bytes 1572872 | tf_op jit(solution)/shard_map/ppermute | solution.py:139
  300.8 275.1 %collective-permute-start.1 = (f32[1024,128]{1,0:T(8,128)S(1)}, f32[1024,128]{1,0:T(8,128)S(1)}, u32[]{:S(2)}, u32[]{:S(2)}) collective-permute-start(f32[1024,128]{1,0:T(8,128)S(1)} %add.471), channel_id=1, source_target_pairs={{0,2},{1,3},{2,0},{3,1},{4,6},{5,7},{6,4},{7,5},{8,10},{9,11},{10,... | collective-permute-start | bytes 1572872 | tf_op jit(solution)/shard_map/ppermute | solution.py:139
  305.6 27.9 %all-to-all-start.3 = ((f32[9,128,8]{0,2,1:T(8,128)}), f32[9,128,8]{0,2,1:T(8,128)S(1)}, u32[]{:S(2)}, u32[]{:S(2)}) async-start(f32[9,128,8]{0,2,1:T(8,128)} %bitcast.13), calls=%async_computation.3 | async-start | bytes 1048576 | tf_op jit(solution)/shard_map/all_to_all | solution.py:131
  (97 other events, 120.9 us)
Sparse Core Ops, SparseCore 0:
  304.0 270.1 all-reduce.10
